TPU v7x, 32 devices: a whole 2x2x4 slice. The times are simulated.
32 devices in a mesh: segment: 2 (over x), expert: 16 (over z, y, core).
Axes of the slice: x: 2, y: 2, z: 4, core: 2. Of those that a mesh axis runs over, the one named last changes fastest.
Arguments:
- handoff: bfloat16 [2, 1024, 4096], P('segment', 'expert'), may hold values from -6 to 6
- saved_inputs: bfloat16 [2, 1024, 4096], P('segment', 'expert'), may hold values from -6 to 6
- cotangent: bfloat16 [2, 1024, 4096], P('segment', 'expert'), may hold values from -6 to 6
- ids_forward: int32 [2, 1024, 2], P('segment', 'expert'), may hold values from 0 to 63, all different within a row; in each aligned block of 64 rows (0 to 63, 64 to 127, ..., all dimensions but the last counted through in order) at most 5 rows name the same one
- gates_forward: float32 [2, 1024, 2], P('segment', 'expert'), may hold values from 0.25 to 1
- ids_backward: int32 [2, 1024, 2], P('segment', 'expert'), may hold values from 0 to 63, all different within a row; in each aligned block of 64 rows (0 to 63, 64 to 127, ..., all dimensions but the last counted through in order) at most 5 rows name the same one
- gates_backward: float32 [2, 1024, 2], P('segment', 'expert'), may hold values from 0.25 to 1
- weight_in: bfloat16 [2, 4096, 2048], P('segment', None, 'expert'), may hold values from -0.09375 to 0.09375
- weight_out: bfloat16 [2, 2048, 4096], P('segment', 'expert'), may hold values from -0.125 to 0.125
Outputs:
- expert_mix: bfloat16 [2, 1024, 4096], P('segment', 'expert')
- input_grads: bfloat16 [2, 1024, 4096], P('segment', 'expert')
Inputs may be any that keep to these rules, and one draw needn't show every extreme that they name: `ids_forward`: the two experts of a row differ; within the rows of one device no expert is named by more than 5 rows. `ids_backward`: the two experts of a row differ; within the rows of one device no expert is named by more than 5 rows.
All inputs are finite; a program needn't handle non-finite values.
Results may differ from a plain program's by a relative error of at most 0.013.
Values may be sent and summed in bfloat16 or wider, within the bound.
A program may use at most 128 MiB of HBM per device.

v0:
```python
import jax
import jax.numpy as jnp
from jax import lax
from jax.sharding import PartitionSpec as P

GROUP = 16
CAP = 5


def shifted(block, axis, distance):
    devices = range(lax.axis_size(axis))
    route = [(i - distance, i) for i in devices if i - distance in devices]
    return lax.ppermute(block, axis, route)


def slot_tables(expert_ids, gate_values, experts):
    row_count = expert_ids.shape[0]
    flat_ids = expert_ids.reshape(row_count * 2)
    window = jnp.arange(experts, dtype=jnp.int32)
    member = (flat_ids[None, :] == window[:, None]).astype(jnp.int32)
    before = jnp.cumsum(member, axis=1, dtype=jnp.int32) - member
    positions = jnp.arange(CAP, dtype=jnp.int32)
    picked_slots = (
        member[:, None, :] * (before[:, None, :] == positions[None, :, None]).astype(jnp.int32)
    ).astype(jnp.float32)
    picked_slots = picked_slots.reshape(experts * CAP, row_count, 2)
    select = jnp.sum(picked_slots, axis=2)
    weighted = jnp.sum(picked_slots * gate_values[None, :, :], axis=2)
    return (select, weighted)


def pack_direct(stacked, groups):
    stacks = stacked.shape[0]
    feature_width = stacked.shape[2]
    shaped = stacked.reshape(stacks, groups, 1, CAP, feature_width)
    spread_out = jnp.broadcast_to(shaped, (stacks, groups, GROUP, CAP, feature_width))
    return spread_out.reshape(stacks, groups * GROUP, CAP, feature_width)


def expert_forward(arriving, local_in, local_out):
    feature_width = arriving.shape[-1]
    preact = jnp.dot(
        arriving.reshape(-1, feature_width), local_in, preferred_element_type=jnp.float32
    )
    hidden = jax.nn.silu(preact).astype(jnp.bfloat16)
    partial_out = jnp.dot(hidden, local_out, preferred_element_type=jnp.float32).astype(
        jnp.bfloat16
    )
    return partial_out.reshape(arriving.shape)


def expert_backward(row_part, grad_part, local_in, local_out):
    feature_width = row_part.shape[-1]
    preact = jnp.dot(
        row_part.reshape(-1, feature_width), local_in, preferred_element_type=jnp.float32
    )
    sigmoid_v = jax.nn.sigmoid(preact)
    slope_v = sigmoid_v * (1.0 + preact * (1.0 - sigmoid_v))
    grad_hidden = jnp.einsum(
        "rd,hd->rh",
        grad_part.reshape(-1, feature_width),
        local_out,
        preferred_element_type=jnp.float32,
    )
    grad_pre = (grad_hidden * slope_v).astype(jnp.bfloat16)
    partial_grad = jnp.einsum(
        "rh,dh->rd", grad_pre, local_in, preferred_element_type=jnp.float32
    ).astype(jnp.bfloat16)
    return partial_grad.reshape(row_part.shape)


def gather_groups(returned, groups):
    feature_width = returned.shape[-1]
    summed = jnp.sum(
        returned.reshape(groups, GROUP, CAP, feature_width).astype(jnp.float32), axis=1
    )
    return summed.reshape(groups * CAP, feature_width)


def per_device(
    handoff,
    saved_inputs,
    cotangent,
    ids_forward,
    gates_forward,
    ids_backward,
    gates_backward,
    weight_in,
    weight_out,
):
    highest = lax.Precision.HIGHEST
    groups = lax.axis_size("expert") // GROUP
    segment_index = lax.axis_index("segment")
    last_segment = lax.axis_size("segment") - 1
    arrived = shifted(handoff, "segment", 1)
    inputs = jnp.where(segment_index == 0, handoff, arrived)[0]
    returned = shifted(cotangent, "segment", -1)
    upstream = jnp.where(segment_index == last_segment, cotangent, returned)[0]
    local_in = weight_in[0]
    local_out = weight_out[0]
    select_f, weigh_f = slot_tables(ids_forward[0], gates_forward[0], groups)
    picked = jnp.dot(
        select_f.astype(jnp.bfloat16), inputs, preferred_element_type=jnp.float32
    ).astype(jnp.bfloat16)
    select_b, weigh_b = slot_tables(ids_backward[0], gates_backward[0], groups)
    rows_back = jnp.dot(
        select_b.astype(jnp.bfloat16), saved_inputs[0], preferred_element_type=jnp.float32
    ).astype(jnp.bfloat16)
    grads_out = jnp.dot(
        weigh_b, upstream.astype(jnp.float32), precision=highest, preferred_element_type=jnp.float32
    ).astype(jnp.bfloat16)
    backward_stack = jnp.stack([rows_back, grads_out])
    arriving_f = lax.all_to_all(
        pack_direct(picked[None], groups), "expert", split_axis=1, concat_axis=1, tiled=True
    )
    arriving_b = lax.all_to_all(
        pack_direct(backward_stack, groups), "expert", split_axis=1, concat_axis=1, tiled=True
    )
    partial_f = expert_forward(arriving_f[0], local_in, local_out)
    back_f = lax.all_to_all(partial_f, "expert", split_axis=0, concat_axis=0, tiled=True)
    combined = gather_groups(back_f, groups)
    expert_mix = jnp.dot(
        weigh_f.T, combined, precision=highest, preferred_element_type=jnp.float32
    ).astype(jnp.bfloat16)
    partial_b = expert_backward(arriving_b[0], arriving_b[1], local_in, local_out)
    back_b = lax.all_to_all(partial_b, "expert", split_axis=0, concat_axis=0, tiled=True)
    slot_grads = gather_groups(back_b, groups)
    input_grads = jnp.dot(
        select_b.T, slot_grads, precision=highest, preferred_element_type=jnp.float32
    ).astype(jnp.bfloat16)
    return (expert_mix[None], input_grads[None])


def solution(mesh):
    return jax.shard_map(
        per_device,
        mesh=mesh,
        in_specs=(
            P("segment", "expert", None),
            P("segment", "expert", None),
            P("segment", "expert", None),
            P("segment", "expert", None),
            P("segment", "expert", None),
            P("segment", "expert", None),
            P("segment", "expert", None),
            P("segment", None, "expert"),
            P("segment", "expert", None),
        ),
        out_specs=(P("segment", "expert", None), P("segment", "expert", None)),
        check_vma=False,
    )
```

profile of v0, /device:TPU:0, one launch (start us, length us, event | category | flops | bytes accessed | tf_op | source)
XLA Modules:
  0.0 150.6 jit_solution(6945938500886231329)
XLA Ops:
  0.6 0.0 copy-start
  0.6 1.4 collective-permute-start.1
  2.1 5.7 %collective-permute-start = (bf16[1,64,4096]{2,1,0:T(8,128)(2,1)}, bf16[1,64,4096]{2,1,0:T(8,128)(2,1)S(1)}, u32[]{:S(2)}, u32[]{:S(2)}) collective-permute-start(bf16[1,64,4096]{2,1,0:T(8,128)(2,1)} %param.9), channel_id=1, source_target_pairs={{0,16},{1,17},{2,18},{3,19},{4,20},{5,21},{6,22},{7,23},{8,24},{9,... | collective-permute-start | bytes 1572872 | tf_op jit(solution)/shard_map/ppermute | solution.py:13
  7.8 0.7 compare_convert_fusion.1
  8.5 0.1 copy.43
  8.6 0.1 reshape.191
  8.7 0.3 reduce_window_sum.21
  9.0 0.5 broadcast.125
  9.5 0.7 reduce.14
  10.2 0.1 reduce_window_sum.22
  10.4 0.1 copy.44
  10.4 0.7 bitcast_subtract_fusion.1
  11.1 0.7 fusion.37
  11.8 7.5 %collective-permute-done = bf16[1,64,4096]{2,1,0:T(8,128)(2,1)S(1)} collective-permute-done((bf16[1,64,4096]{2,1,0:T(8,128)(2,1)}, bf16[1,64,4096]{2,1,0:T(8,128)(2,1)S(1)}, u32[]{:S(2)}, u32[]{:S(2)}) %collective-permute-start) | collective-permute-done | bytes 524320 | tf_op jit(solution)/shard_map/ppermute | solution.py:13
  19.3 1.2 convolution_convert_fusion.6
  20.5 1.1 reshape.187
  21.6 6.9 %all-to-all-start = ((bf16[1,16,5,4096]{3,2,0,1:T(8,128)(2,1)}), bf16[1,16,5,4096]{3,2,0,1:T(8,128)(2,1)S(1)}, u32[]{:S(2)}, u32[]{:S(2)}) async-start(bf16[1,16,5,4096]{3,2,0,1:T(8,128)(2,1)} %reshape.187), calls=%async_computation | async-start | bytes 2097152 | tf_op jit(solution)/shard_map/all_to_all | solution.py:113
  28.6 0.1 copy.45
  28.7 0.1 reshape.193
  28.8 0.3 reduce_window_sum.23
  29.1 0.7 reduce.15
  29.8 0.1 reduce_window_sum.24
  29.9 0.1 copy.46
  30.0 0.2 fusion.2
  30.2 1.4 fusion.3
  31.7 0.1 copy.47
  31.8 19.7 %all-to-all-done = bf16[1,16,5,4096]{3,2,0,1:T(8,128)(2,1)S(1)} async-done(((bf16[1,16,5,4096]{3,2,0,1:T(8,128)(2,1)}), bf16[1,16,5,4096]{3,2,0,1:T(8,128)(2,1)S(1)}, u32[]{:S(2)}, u32[]{:S(2)}) %all-to-all-start) | async-done | bytes 655392 | tf_op jit(solution)/shard_map/all_to_all | solution.py:113
  51.4 2.4 %reshape.189 = bf16[2,16,5,4096]{3,0,2,1:T(2,128)(2,1)} broadcast(bf16[2,5,4096]{2,0,1:T(2,128)(2,1)S(1)} %copy.47), dimensions={0,2,3} | broadcast | bytes 1392640 | tf_op jit(solution)/shard_map/reshape | solution.py:37
  53.8 6.8 %all-to-all-start.2 = ((bf16[2,16,5,4096]{3,0,2,1:T(2,128)(2,1)}), bf16[2,16,5,4096]{3,0,2,1:T(2,128)(2,1)S(1)}, u32[]{:S(2)}, u32[]{:S(2)}) async-start(bf16[2,16,5,4096]{3,0,2,1:T(2,128)(2,1)} %reshape.189), calls=%async_computation.2 | async-start | bytes 2621440 | tf_op jit(solution)/shard_map/all_to_all | solution.py:116
  60.6 0.0 copy-start.1
  60.6 2.4 %reshape_squeeze.9 = bf16[80,4096]{1,0:T(8,128)(2,1)} reshape(bf16[1,16,5,4096]{3,2,0,1:T(8,128)(2,1)} %copy-done.2) | data formatting | bytes 1310720 | tf_op jit(solution)/shard_map/reshape;squeeze | solution.py:43
  63.0 2.6 %convolution_convert_fusion.1 = bf16[80,4096]{1,0:T(8,128)(2,1)} fusion(bf16[1,128,4096]{2,1,0:T(8,128)(2,1)S(1)} %copy-done.1, bf16[80,4096]{1,0:T(8,128)(2,1)} %reshape_squeeze.9, bf16[1,4096,128]{2,1,0:T(8,128)(2,1)S(1)} %copy-done), kind=kOutput, calls=%fused_computation.1 | convolution fusion | flops 168151040 | bytes 3407872 | tf_op jit(solution)/shard_map/dot_general | solution.py:46
  65.6 2.3 %reshape.188 = bf16[16,5,4096]{2,1,0:T(8,128)(2,1)} reshape(bf16[80,4096]{1,0:T(8,128)(2,1)} %convolution_convert_fusion.1) | data formatting | bytes 1310720 | tf_op jit(solution)/shard_map/reshape | solution.py:49
  67.9 19.9 %all-to-all-done.2 = bf16[2,16,5,4096]{3,0,2,1:T(2,128)(2,1)S(1)} async-done(((bf16[2,16,5,4096]{3,0,2,1:T(2,128)(2,1)}), bf16[2,16,5,4096]{3,0,2,1:T(2,128)(2,1)S(1)}, u32[]{:S(2)}, u32[]{:S(2)}) %all-to-all-start.2) | async-done | bytes 1310752 | tf_op jit(solution)/shard_map/all_to_all | solution.py:116
  87.9 8.1 %all-to-all-start.1 = ((bf16[16,5,4096]{2,1,0:T(8,128)(2,1)}), bf16[16,5,4096]{2,1,0:T(8,128)(2,1)}, u32[]{:S(2)}, u32[]{:S(2)}) async-start(bf16[16,5,4096]{2,1,0:T(8,128)(2,1)} %reshape.188), calls=%async_computation.1 | async-start | bytes 2097152 | tf_op jit(solution)/shard_map/all_to_all | solution.py:120
  96.0 7.1 %slice_reduce_fusion = (bf16[16,5,4096]{2,1,0:T(8,128)(2,1)}, bf16[16,5,4096]{2,1,0:T(8,128)(2,1)}) fusion(bf16[2,16,5,4096]{3,0,2,1:T(2,128)(2,1)S(1)} %all-to-all-done.2), kind=kLoop, calls=%fused_computation.13 | loop fusion | bytes 2621440 | tf_op jit(solution)/shard_map/slice | solution.py:125
  103.0 2.4 %reshape_squeeze.11 = bf16[80,4096]{1,0:T(8,128)(2,1)} reshape(bf16[16,5,4096]{2,1,0:T(8,128)(2,1)} %get-tuple-element.2) | data formatting | bytes 1310720 | tf_op jit(solution)/shard_map/reshape;squeeze | solution.py:55
  105.5 1.1 reshape_squeeze.10
  106.6 1.5 fusion.9
  108.1 1.3 convolution_convert_fusion
  109.4 1.2 reshape.190
  110.7 8.2 %all-to-all-done.1 = bf16[16,5,4096]{2,1,0:T(8,128)(2,1)} async-done(((bf16[16,5,4096]{2,1,0:T(8,128)(2,1)}), bf16[16,5,4096]{2,1,0:T(8,128)(2,1)}, u32[]{:S(2)}, u32[]{:S(2)}) %all-to-all-start.1) | async-done | bytes 655392 | tf_op jit(solution)/shard_map/all_to_all | solution.py:120
  118.9 6.8 %all-to-all-start.3 = ((bf16[16,5,4096]{2,1,0:T(8,128)(2,1)}), bf16[16,5,4096]{2,1,0:T(8,128)(2,1)S(1)}, u32[]{:S(2)}, u32[]{:S(2)}) async-start(bf16[16,5,4096]{2,1,0:T(8,128)(2,1)} %reshape.190), calls=%async_computation.3 | async-start | bytes 2097152 | tf_op jit(solution)/shard_map/all_to_all | solution.py:126
  125.7 1.4 convert_reduce_fusion.1
  127.1 1.8 %fusion = bf16[1,64,4096]{2,1,0:T(8,128)(2,1)} fusion(f32[5,64]{1,0:T(8,128)S(1)} %get-tuple-element.7, f32[5,4096]{1,0:T(8,128)S(1)} %convert_reduce_fusion.1), kind=kOutput, calls=%fused_computation.4 | convolution fusion | flops 15990784 | bytes 607488 | tf_op jit(solution)/shard_map/dot_general | solution.py:122
  129.0 19.6 %all-to-all-done.3 = bf16[16,5,4096]{2,1,0:T(8,128)(2,1)S(1)} async-done(((bf16[16,5,4096]{2,1,0:T(8,128)(2,1)}), bf16[16,5,4096]{2,1,0:T(8,128)(2,1)S(1)}, u32[]{:S(2)}, u32[]{:S(2)}) %all-to-all-start.3) | async-done | bytes 655392 | tf_op jit(solution)/shard_map/all_to_all | solution.py:126
  148.6 0.2 convert_reduce_fusion
  148.8 1.8 %fusion.1 = bf16[1,64,4096]{2,1,0:T(8,128)(2,1)} fusion(f32[5,64]{1,0:T(8,128)S(1)} %get-tuple-element.5, f32[5,4096]{1,0:T(8,128)S(1)} %convert_reduce_fusion), kind=kOutput, calls=%fused_computation.5 | convolution fusion | flops 15990784 | bytes 607488 | tf_op jit(solution)/shard_map/dot_general | solution.py:128
  (21 shorter events, 0.1 us)
Async XLA Ops:
  0.6 62.4 %copy-start = (bf16[1,4096,128]{2,1,0:T(8,128)(2,1)S(1)}, bf16[1,4096,128]{2,1,0:T(8,128)(2,1)}, u32[]{:S(2)}) copy-start(bf16[1,4096,128]{2,1,0:T(8,128)(2,1)} %param.16) | copy-start | bytes 3145732
  0.6 29.6 %collective-permute-start.1 = (bf16[1,64,4096]{2,1,0:T(8,128)(2,1)}, bf16[1,64,4096]{2,1,0:T(8,128)(2,1)}, u32[]{:S(2)}, u32[]{:S(2)}) collective-permute-start(bf16[1,64,4096]{2,1,0:T(8,128)(2,1)} %param.11), channel_id=1, source_target_pairs={{16,0},{17,1},{18,2},{19,3},{20,4},{21,5},{22,6},{23,7},{24,8},{25... | collective-permute-start | bytes 1572872 | tf_op jit(solution)/shard_map/ppermute | solution.py:13
  2.1 17.2 %collective-permute-start = (bf16[1,64,4096]{2,1,0:T(8,128)(2,1)}, bf16[1,64,4096]{2,1,0:T(8,128)(2,1)S(1)}, u32[]{:S(2)}, u32[]{:S(2)}) collective-permute-start(bf16[1,64,4096]{2,1,0:T(8,128)(2,1)} %param.9), channel_id=1, source_target_pairs={{0,16},{1,17},{2,18},{3,19},{4,20},{5,21},{6,22},{7,23},{8,24},{9,... | collective-permute-start | bytes 1572872 | tf_op jit(solution)/shard_map/ppermute | solution.py:13
  21.6 6.9 %copy-start.7 = (s32[1,64,2]{1,2,0:T(2,128)S(1)}, s32[1,64,2]{1,2,0:T(2,128)}, u32[]{:S(2)}) copy-start(s32[1,64,2]{1,2,0:T(2,128)} %param.14) | copy-start | bytes 1540
  21.6 8.4 %copy-start.8 = (f32[1,64,2]{1,2,0:T(2,128)S(1)}, f32[1,64,2]{1,2,0:T(2,128)}, u32[]{:S(2)}) copy-start(f32[1,64,2]{1,2,0:T(2,128)} %param.15) | copy-start | bytes 1540
  21.6 8.4 %copy-start.5 = (bf16[1,64,4096]{2,1,0:T(8,128)(2,1)S(1)}, bf16[1,64,4096]{2,1,0:T(8,128)(2,1)}, u32[]{:S(2)}) copy-start(bf16[1,64,4096]{2,1,0:T(8,128)(2,1)} %param.10) | copy-start | bytes 1572868
  21.6 8.6 %copy-start.6 = (bf16[1,64,4096]{2,1,0:T(8,128)(2,1)S(1)}, bf16[1,64,4096]{2,1,0:T(8,128)(2,1)}, u32[]{:S(2)}) copy-start(bf16[1,64,4096]{2,1,0:T(8,128)(2,1)} %param.11) | copy-start | bytes 1572868
  21.6 29.8 %all-to-all-start = ((bf16[1,16,5,4096]{3,2,0,1:T(8,128)(2,1)}), bf16[1,16,5,4096]{3,2,0,1:T(8,128)(2,1)S(1)}, u32[]{:S(2)}, u32[]{:S(2)}) async-start(bf16[1,16,5,4096]{3,2,0,1:T(8,128)(2,1)} %reshape.187), calls=%async_computation | async-start | bytes 2097152 | tf_op jit(solution)/shard_map/all_to_all | solution.py:113
  51.4 2.4 %copy-start.2 = (bf16[1,16,5,4096]{3,2,0,1:T(8,128)(2,1)}, bf16[1,16,5,4096]{3,2,0,1:T(8,128)(2,1)S(1)}, u32[]{:S(2)}) copy-start(bf16[1,16,5,4096]{3,2,0,1:T(8,128)(2,1)S(1)} %all-to-all-done) | copy-start | bytes 1966084
  53.8 34.1 %all-to-all-start.2 = ((bf16[2,16,5,4096]{3,0,2,1:T(2,128)(2,1)}), bf16[2,16,5,4096]{3,0,2,1:T(2,128)(2,1)S(1)}, u32[]{:S(2)}, u32[]{:S(2)}) async-start(bf16[2,16,5,4096]{3,0,2,1:T(2,128)(2,1)} %reshape.189), calls=%async_computation.2 | async-start | bytes 2621440 | tf_op jit(solution)/shard_map/all_to_all | solution.py:116
  60.6 2.4 %copy-start.1 = (bf16[1,128,4096]{2,1,0:T(8,128)(2,1)S(1)}, bf16[1,128,4096]{2,1,0:T(8,128)(2,1)}, u32[]{:S(2)}) copy-start(bf16[1,128,4096]{2,1,0:T(8,128)(2,1)} %param.17) | copy-start | bytes 3145732
  87.9 31.0 %all-to-all-start.1 = ((bf16[16,5,4096]{2,1,0:T(8,128)(2,1)}), bf16[16,5,4096]{2,1,0:T(8,128)(2,1)}, u32[]{:S(2)}, u32[]{:S(2)}) async-start(bf16[16,5,4096]{2,1,0:T(8,128)(2,1)} %reshape.188), calls=%async_computation.1 | async-start | bytes 2097152 | tf_op jit(solution)/shard_map/all_to_all | solution.py:120
  103.0 2.4 %copy-start.3 = (bf16[16,5,4096]{2,1,0:T(8,128)(2,1)S(1)}, bf16[16,5,4096]{2,1,0:T(8,128)(2,1)}, u32[]{:S(2)}) copy-start(bf16[16,5,4096]{2,1,0:T(8,128)(2,1)} %get-tuple-element.3) | copy-start | bytes 1966084
  106.6 1.5 copy-start.4
  118.9 29.7 %all-to-all-start.3 = ((bf16[16,5,4096]{2,1,0:T(8,128)(2,1)}), bf16[16,5,4096]{2,1,0:T(8,128)(2,1)S(1)}, u32[]{:S(2)}, u32[]{:S(2)}) async-start(bf16[16,5,4096]{2,1,0:T(8,128)(2,1)} %reshape.190), calls=%async_computation.3 | async-start | bytes 2097152 | tf_op jit(solution)/shard_map/all_to_all | solution.py:126
where the time goes:
time: 153 us; the launch traced here: 151 us
  waiting for transfers between devices  74.9 us (49%)
  starting transfers between devices  35.7 us (23%)
  local copies, waits for them, and re-layouts  21.6 us (14%)
  matrix products  11.8 us (8%)
  other arithmetic  5.76 us (4%)
    all_to_all x1, waiting for transfers between devices, per_device(): lax.all_to_all(pack_direct(backward_stack, groups), 'expert', split_axis=...  19.9 us
    all_to_all x1, waiting for transfers between devices, per_device(): lax.all_to_all(pack_direct(picked[None], groups), 'expert', split_axis=1,...  19.7 us
    all_to_all x1, waiting for transfers between devices, per_device(): lax.all_to_all(partial_b, 'expert', split_axis=0, concat_axis=0, tiled=True)  19.6 us
    all_to_all x1, waiting for transfers between devices, per_device(): lax.all_to_all(partial_f, 'expert', split_axis=0, concat_axis=0, tiled=True)  8.23 us
    all_to_all x1, starting transfers between devices, per_device(): lax.all_to_all(partial_f, 'expert', split_axis=0, concat_axis=0, tiled=True)  8.08 us
    ppermute x2, waiting for transfers between devices, shifted(): return lax.ppermute(block, axis, route)  7.47 us
    ppermute x2, starting transfers between devices, shifted(): return lax.ppermute(block, axis, route)  7.14 us
    slice x1, local copies, waits for them, and re-layouts, per_device(): arriving_b[0]  7.07 us
  transfers between devices with their start and end apart: 6, of which 5 were waited for; matrix products, arithmetic and copies ran while one was open for 23% of the time, Pallas kernels for 0%

commit v1 on v0

--- a/solution.py
+++ b/solution.py
@@ -1,6 +1,10 @@
+import functools
+
 import jax
 import jax.numpy as jnp
 from jax import lax
+from jax.experimental import pallas as pl
+from jax.experimental.pallas import tpu as pltpu
 from jax.sharding import PartitionSpec as P
 
 GROUP = 16
@@ -131,9 +135,405 @@
     return (expert_mix[None], input_grads[None])
 
 
+MESH = pl.DeviceIdType.MESH
+BLOCK = 16
+LANES = 128
+
+
+def flipped(position, mask):
+    bit = 1
+    while bit <= mask:
+        if mask & bit:
+            position = position + bit * (1 - 2 * ((position // bit) % 2))
+        bit *= 2
+    return position
+
+
+def exchange_kernel(
+    planes,
+    wire,
+    ids_f,
+    gates_f,
+    ids_b,
+    gates_b,
+    handoff,
+    saved,
+    cotangent,
+    weight_in,
+    weight_out,
+    out_f,
+    out_b,
+    rows_x,
+    rows_s,
+    w_in_side,
+    w_out_side,
+    blocks,
+    req_send,
+    req_recv,
+    resp_send,
+    resp_recv,
+    own_rows,
+    pair_send,
+    pair_keep,
+    pair_recv,
+    y_send,
+    y_keep,
+    y_recv,
+    z_send,
+    z_recv,
+    own_sum,
+    local_sem,
+    send_sem,
+    recv_sem,
+):
+    segment = lax.axis_index("segment")
+    expert = lax.axis_index("expert")
+    row_count, width = rows_x.shape
+    tail_width = width - wire
+    hidden = weight_out.shape[0]
+
+    def at_expert(mask):
+        return {"expert": flipped(expert, mask)}
+
+    other_segment = {"segment": 1 - segment}
+    sibling = at_expert(1)
+    across = at_expert(2)
+    mates = [None] + [at_expert(4 * k) for k in range(1, planes)]
+
+    barrier = pltpu.get_barrier_semaphore()
+    partners = [other_segment, sibling, across] + mates[1:]
+    for partner in partners:
+        pl.semaphore_signal(barrier, inc=1, device_id=partner, device_id_type=MESH)
+
+    @pl.when(segment == 0)
+    def _():
+        pltpu.make_async_copy(handoff, rows_x, local_sem.at[0]).start()
+
+    @pl.when(segment != 0)
+    def _():
+        pltpu.make_async_copy(cotangent, rows_x, local_sem.at[0]).start()
+
+    load_x = pltpu.make_async_copy(handoff, rows_x, local_sem.at[0])
+    load_s = pltpu.make_async_copy(saved, rows_s, local_sem.at[1])
+    load_in = pltpu.make_async_copy(weight_in, w_in_side.at[:, 0:hidden], local_sem.at[2])
+    load_out = pltpu.make_async_copy(weight_out, w_out_side.at[0:hidden, :], local_sem.at[3])
+    load_s.start()
+    load_in.start()
+    load_out.start()
+
+    count = [0]
+    started = []
+
+    def remote(source, target, device):
+        number = count[0]
+        count[0] += 1
+        return pltpu.make_async_remote_copy(
+            src_ref=source,
+            dst_ref=target,
+            send_sem=send_sem.at[number],
+            recv_sem=recv_sem.at[number],
+            device_id=device,
+            device_id_type=MESH,
+        )
+
+    def begin(copy):
+        copy.start()
+        started.append(copy)
+
+    request = remote(req_send, req_recv, other_segment)
+    response = remote(resp_send, resp_recv, other_segment)
+    gather_z = [None] + [remote(blocks.at[0, 0, 0], blocks.at[k, 0, 0], mates[k]) for k in range(1, planes)]
+    gather_y = [remote(blocks.at[k, 0, 0], blocks.at[k, 1, 0], across) for k in range(planes)]
+    gather_c0 = [remote(blocks.at[k, 0, 0], blocks.at[k, 0, 1], sibling) for k in range(planes)]
+    gather_c1 = [remote(blocks.at[k, 1, 0], blocks.at[k, 1, 1], sibling) for k in range(planes)]
+    reduce_c = [remote(pair_send.at[k], pair_recv.at[k], sibling) for k in range(planes)]
+    reduce_y = [remote(y_send.at[k], y_recv.at[k], across) for k in range(planes)]
+    reduce_z = [None] + [remote(z_send.at[k], z_recv.at[k], mates[k]) for k in range(1, planes)]
+
+    def ranks(ids, gates):
+        first, second = ids[:, 0:1] == 0, ids[:, 1:2] == 0
+        member = jnp.where(first | second, 1.0, 0.0)
+        gate = jnp.where(first, gates[:, 0:1], 0.0) + jnp.where(second, gates[:, 1:2], 0.0)
+        earlier = lax.broadcasted_iota(jnp.int32, (row_count, row_count), 1) < lax.broadcasted_iota(
+            jnp.int32, (row_count, row_count), 0
+        )
+        wide = jnp.broadcast_to(member, (row_count, LANES))
+        rank = jnp.dot(
+            jnp.where(earlier, 1.0, 0.0).astype(jnp.bfloat16),
+            wide.astype(jnp.bfloat16),
+            preferred_element_type=jnp.float32,
+        )
+        return wide, rank.astype(jnp.int32), jnp.broadcast_to(gate, (row_count, LANES))
+
+    lane = lax.broadcasted_iota(jnp.int32, (row_count, LANES), 1)
+
+    def placed(member, rank, offset, at=lane):
+        slot = at - offset
+        fits = (slot == rank) & (slot < CAP) & (slot >= 0)
+        return jnp.where(fits, member, 0.0)
+
+    member_f, rank_f, gate_f = ranks(ids_f, gates_f)
+    member_b, rank_b, gate_b = ranks(ids_b, gates_b)
+    table = (
+        placed(member_f, rank_f, 0)
+        + placed(member_b, rank_b, CAP)
+        + placed(member_b, rank_b, 2 * CAP) * gate_b
+    )
+    unit = jnp.where(
+        lax.broadcasted_iota(jnp.int32, (BLOCK, LANES), 0)
+        == lax.broadcasted_iota(jnp.int32, (BLOCK, LANES), 1),
+        1.0,
+        0.0,
+    )
+    by_slot = lax.dot_general(
+        unit,
+        table,
+        (((1,), (1,)), ((), ())),
+        precision=lax.Precision.HIGHEST,
+        preferred_element_type=jnp.float32,
+    )
+    slot_row = lax.broadcasted_iota(jnp.int32, (BLOCK, row_count), 0)
+
+    def rows_from(low):
+        return jnp.where((slot_row >= low) & (slot_row < low + CAP), by_slot, 0.0)
+
+    asked = rows_from((1 - segment) * (2 * CAP))
+    mine = rows_from(segment * (2 * CAP))
+    kept = rows_from(CAP)
+    req_send[...] = jnp.concatenate([asked, jnp.zeros((BLOCK, LANES - row_count), jnp.float32)], axis=1)
+    pl.semaphore_wait(barrier, len(partners))
+    begin(request)
+
+    def picked(weights, rows_ref):
+        scale = jnp.sum(weights, axis=1, keepdims=True)
+        choose = jnp.where(weights != 0.0, 1.0, 0.0).astype(jnp.bfloat16)
+        return jnp.dot(choose, rows_ref[...], preferred_element_type=jnp.float32) * scale
+
+    load_x.wait()
+    load_s.wait()
+    own_rows[...] = picked(mine, rows_x) + picked(kept, rows_s)
+    request.wait_recv()
+    resp_send[...] = picked(req_recv[:, 0:row_count], rows_x).astype(jnp.bfloat16)
+    begin(response)
+    load_in.wait()
+    load_out.wait()
+    turn = 512 if width % 512 == 0 else LANES
+
+    def transposes(step, carry):
+        piece = pl.ds(pl.multiple_of(step * turn, turn), turn)
+        w_in_side[piece, hidden : 2 * hidden] = w_out_side[0:hidden, piece].T
+        w_out_side[hidden : 2 * hidden, piece] = w_in_side[piece, 0:hidden].T
+        return carry
+
+    lax.fori_loop(0, width // turn, transposes, 0)
+    response.wait_recv()
+    blocks[0, 0, 0] = (own_rows[...] + resp_recv[...].astype(jnp.float32)).astype(jnp.bfloat16)
+
+    def spread(k):
+        if k > 0:
+            gather_z[k].wait_recv()
+        begin(gather_y[k])
+        begin(gather_c0[k])
+
+    def relay(k):
+        gather_y[k].wait_recv()
+        begin(gather_c1[k])
+
+    batch = 4 * BLOCK
+    place = lax.broadcasted_iota(jnp.int32, (batch, hidden), 0) % BLOCK
+    chunk = 256 if tail_width % 256 == 0 and wire % 256 == 0 else LANES
+
+    def compute(k):
+        gather_c0[k].wait_recv()
+        gather_c1[k].wait_recv()
+
+        def contract(step, total):
+            piece = pl.ds(pl.multiple_of(step * turn, turn), turn)
+            return total + jnp.dot(
+                blocks[k, :, :, :, piece].reshape(batch, turn),
+                w_in_side[piece, :],
+                preferred_element_type=jnp.float32,
+            )
+
+        both = lax.fori_loop(
+            0, width // turn, contract, jnp.zeros((batch, 2 * hidden), jnp.float32), unroll=True
+        )
+        pre = both[:, 0:hidden]
+        grad_hidden = pltpu.roll(both[:, hidden:], batch - CAP, 0)
+        gate = 1.0 / (1.0 + jnp.exp(-pre))
+        forward = jnp.where(place < CAP, pre * gate, 0.0)
+        slope = gate * (1.0 + pre * (1.0 - gate))
+        backward = jnp.where((place >= CAP) & (place < 2 * CAP), grad_hidden * slope, 0.0)
+        late_f = pltpu.roll(forward, 2 * CAP, 0).astype(jnp.bfloat16)
+        late_b = pltpu.roll(backward, CAP, 0).astype(jnp.bfloat16)
+        main = jnp.concatenate([forward, backward], axis=1).astype(jnp.bfloat16)
+
+        def put(start, value):
+            columns = pl.ds(start, chunk)
+            value = value.reshape(2, 2, BLOCK, chunk)
+            pair_keep[k, :, :, columns] = value[:, 0]
+            pair_send[k, :, :, columns] = value[:, 1].astype(jnp.bfloat16)
+
+        def product(start):
+            return jnp.dot(main, w_out_side[:, pl.ds(start, chunk)], preferred_element_type=jnp.float32)
+
+        def pieces(step, carry):
+            start = pl.multiple_of(step * chunk, chunk)
+            late = pl.ds(pl.multiple_of(wire + step * chunk, chunk), chunk)
+            put(
+                start,
+                product(start)
+                + jnp.dot(late_f, w_out_side[0:hidden, late], preferred_element_type=jnp.float32),
+            )
+            start = pl.multiple_of(tail_width + step * chunk, chunk)
+            put(
+                start,
+                product(start)
+                + jnp.dot(
+                    late_b, w_out_side[hidden : 2 * hidden, late], preferred_element_type=jnp.float32
+                ),
+            )
+            return carry
+
+        lax.fori_loop(0, tail_width // chunk, pieces, 0, unroll=True)
+        for start in range(2 * tail_width, wire, chunk):
+            put(start, product(start))
+        begin(reduce_c[k])
+
+    def join_pair(k):
+        reduce_c[k].wait_recv()
+        y_send[k] = (pair_keep[k, 1] + pair_recv[k, 1].astype(jnp.float32)).astype(jnp.bfloat16)
+        begin(reduce_y[k])
+        y_keep[k] = pair_keep[k, 0] + pair_recv[k, 0].astype(jnp.float32)
+
+    def join_plane(k):
+        reduce_y[k].wait_recv()
+        total = y_keep[k] + y_recv[k].astype(jnp.float32)
+        if k == 0:
+            own_sum[...] = total
+        else:
+            z_send[k] = total.astype(jnp.bfloat16)
+            begin(reduce_z[k])
+
+    for k in range(1, planes):
+        begin(gather_z[k])
+    spread(0)
+    for step in range(planes + 2):
+        if step + 1 < planes:
+            spread(step + 1)
+        if step < planes:
+            relay(step)
+        if 0 <= step - 1 < planes:
+            join_pair(step - 1)
+        if 0 <= step - 2 < planes:
+            join_plane(step - 2)
+        if step < planes:
+            compute(step)
+
+    lane_half = lane % BLOCK
+
+    def spread_out(member, rank, offset):
+        ones = placed(member, rank, offset, lane_half)
+        return jnp.where(lane < 2 * BLOCK, ones, 0.0)[:, 0 : 2 * BLOCK].astype(jnp.bfloat16)
+
+    heads = jnp.concatenate([spread_out(member_f, rank_f, 0), spread_out(member_b, rank_b, CAP)], axis=0)
+    late_rows_f = spread_out(member_f, rank_f, 2 * CAP)
+    late_rows_b = spread_out(member_b, rank_b, 2 * CAP)
+    gate_wide = jnp.concatenate([gate_f] * (chunk // LANES), axis=1)
+    for k in range(1, planes):
+        reduce_z[k].wait_recv()
+
+    def halves(start):
+        columns = slice(start, start + chunk)
+        total = own_sum[:, columns]
+        for k in range(1, planes):
+            total = total + z_recv[k, :, columns].astype(jnp.float32)
+        high = total.astype(jnp.bfloat16)
+        low = (total - high.astype(jnp.float32)).astype(jnp.bfloat16)
+        return jnp.concatenate([high, low], axis=0)
+
+    for start in range(0, wire, chunk):
+        both = halves(start)
+        value = jnp.dot(heads, both, preferred_element_type=jnp.float32)
+        out_f[:, start : start + chunk] = (value[0:row_count] * gate_wide).astype(jnp.bfloat16)
+        out_b[:, start : start + chunk] = value[row_count:].astype(jnp.bfloat16)
+        if start < tail_width:
+            value = jnp.dot(late_rows_f, both, preferred_element_type=jnp.float32) * gate_wide
+            out_f[:, wire + start : wire + start + chunk] = value.astype(jnp.bfloat16)
+        elif start < 2 * tail_width:
+            late = wire + start - tail_width
+            value = jnp.dot(late_rows_b, both, preferred_element_type=jnp.float32)
+            out_b[:, late : late + chunk] = value.astype(jnp.bfloat16)
+    for copy in started:
+        copy.wait_send()
+
+
+def exchange(planes, handoff, saved_inputs, cotangent, ids_forward, gates_forward, ids_backward, gates_backward, weight_in, weight_out):
+    rows, width = handoff.shape[1:]
+    hidden = weight_out.shape[1]
+    tiles = width // LANES
+    wire = -(-2 * tiles // 3) * LANES
+    bf16, f32 = jnp.bfloat16, jnp.float32
+    copies = 2 + 2 * (planes - 1) + 5 * planes
+    vmem = pl.BlockSpec(memory_space=pltpu.VMEM)
+    hbm = pl.BlockSpec(memory_space=pl.ANY)
+    mixed, grads = pl.pallas_call(
+        functools.partial(exchange_kernel, planes, wire),
+        out_shape=[jax.ShapeDtypeStruct((rows, width), bf16)] * 2,
+        in_specs=[vmem] * 4 + [hbm] * 5,
+        out_specs=[vmem] * 2,
+        scratch_shapes=[
+            pltpu.VMEM((rows, width), bf16),
+            pltpu.VMEM((rows, width), bf16),
+            pltpu.VMEM((width, 2 * hidden), bf16),
+            pltpu.VMEM((2 * hidden, width), bf16),
+            pltpu.VMEM((planes, 2, 2, BLOCK, width), bf16),
+            pltpu.VMEM((BLOCK, LANES), f32),
+            pltpu.VMEM((BLOCK, LANES), f32),
+            pltpu.VMEM((BLOCK, width), bf16),
+            pltpu.VMEM((BLOCK, width), bf16),
+            pltpu.VMEM((BLOCK, width), f32),
+            pltpu.VMEM((planes, 2, BLOCK, wire), bf16),
+            pltpu.VMEM((planes, 2, BLOCK, wire), f32),
+            pltpu.VMEM((planes, 2, BLOCK, wire), bf16),
+            pltpu.VMEM((planes, BLOCK, wire), bf16),
+            pltpu.VMEM((planes, BLOCK, wire), f32),
+            pltpu.VMEM((planes, BLOCK, wire), bf16),
+            pltpu.VMEM((planes, BLOCK, wire), bf16),
+            pltpu.VMEM((planes, BLOCK, wire), bf16),
+            pltpu.VMEM((BLOCK, wire), f32),
+            pltpu.SemaphoreType.DMA((4,)),
+            pltpu.SemaphoreType.DMA((copies,)),
+            pltpu.SemaphoreType.DMA((copies,)),
+        ],
+        compiler_params=pltpu.CompilerParams(
+            collective_id=0, has_side_effects=True, vmem_limit_bytes=48 * 1024 * 1024
+        ),
+    )(
+        ids_forward[0],
+        gates_forward[0],
+        ids_backward[0],
+        gates_backward[0],
+        handoff[0],
+        saved_inputs[0],
+        cotangent[0],
+        weight_in[0],
+        weight_out[0],
+    )
+    return (mixed[None], grads[None])
+
+
+def device_body(mesh):
+    segments, experts = mesh.shape["segment"], mesh.shape["expert"]
+    planes = experts // 4
+    if segments == 2 and experts == GROUP and planes & (planes - 1) == 0:
+        return functools.partial(exchange, planes)
+    return per_device
+
+
 def solution(mesh):
     return jax.shard_map(
-        per_device,
+        device_body(mesh),
         mesh=mesh,
         in_specs=(
             P("segment", "expert", None),

time: 153 us -> 55 us (0.36); the launches traced: 151 us -> 54.5 us
  waiting for transfers between devices: 74.9 us -> 0 us
  Pallas kernels: 0 us -> 43.9 us
  starting transfers between devices: 35.7 us -> 0 us
  matrix products: 11.8 us -> 0 us
  local copies, waits for them, and re-layouts: 21.6 us -> 9.96 us
  other arithmetic: 5.76 us -> 0 us
    all_to_all x4 -> x0, waiting for transfers between devices: 67.4 us -> none  [the longest x1 19.9 us: per_device(): lax.all_to_all(pack_direct(backward_stack, groups), 'expert', split_axis=...]
    pallas_call x0 -> x1, Pallas kernels: none -> 43.9 us  [exchange(): pl.pallas_call(functools.partial(exchange_kernel, planes, wire), out_shap...]
    all_to_all x4 -> x0, starting transfers between devices: 28.6 us -> none  [the longest x1 8.08 us: per_device(): lax.all_to_all(partial_f, 'expert', split_axis=0, concat_axis=0, tiled=True)]
    dot_general x8 -> x0, matrix products: 11.8 us -> none  [the longest x1 2.57 us: expert_forward(): jnp.dot(hidden, local_out, preferred_element_type=jnp.float32)]
    unnamed x18 -> x20, local copies, waits for them, and re-layouts: 0.04 us -> 9.58 us
    ppermute x2 -> x0, waiting for transfers between devices: 7.47 us -> none  [shifted(): return lax.ppermute(block, axis, route)]
    ppermute x2 -> x0, starting transfers between devices: 7.14 us -> none  [shifted(): return lax.ppermute(block, axis, route)]
    slice x1 -> x0, local copies, waits for them, and re-layouts: 7.07 us -> none  [per_device(): arriving_b[0]]
  transfers between devices with their start and end apart: 6 -> 0, of which waited for: 5 -> 0; matrix products, arithmetic and copies ran while one was open for 23% -> 0% of each run, Pallas kernels for 0% -> 0%
where the time goes in v1:
time: 55 us; the launch traced here: 54.5 us
  Pallas kernels  43.9 us (80%)
  local copies, waits for them, and re-layouts  9.96 us (18%)
  between operations  0.66 us (1%)
    pallas_call x1, Pallas kernels, exchange(): pl.pallas_call(functools.partial(exchange_kernel, planes, wire), out_shap...  43.9 us
    unnamed x20, local copies, waits for them, and re-layouts  9.58 us

profile of v1, /device:TPU:0, one launch (start us, length us, event | category | flops | bytes accessed | tf_op | source)
XLA Modules:
  0.0 54.5 jit_solution(14460314235438756635)
XLA Ops:
  0.6 0.0 copy-start.5
  0.6 0.7 %copy-done.5 = s32[1,64,2]{1,2,0:T(2,128)S(1)} copy-done((s32[1,64,2]{1,2,0:T(2,128)S(1)}, s32[1,64,2]{1,2,0:T(2,128)}, u32[]{:S(2)}) %copy-start.5) | copy-done | bytes 536
  1.3 0.0 copy-start.6
  1.3 0.1 copy.11.ids_f
  1.4 0.6 %copy-done.6 = f32[1,64,2]{1,2,0:T(2,128)S(1)} copy-done((f32[1,64,2]{1,2,0:T(2,128)S(1)}, f32[1,64,2]{1,2,0:T(2,128)}, u32[]{:S(2)}) %copy-start.6) | copy-done | bytes 536
  2.0 0.0 copy-start.7
  2.0 0.1 copy.12.gates_f
  2.1 0.6 %copy-done.7 = s32[1,64,2]{1,2,0:T(2,128)S(1)} copy-done((s32[1,64,2]{1,2,0:T(2,128)S(1)}, s32[1,64,2]{1,2,0:T(2,128)}, u32[]{:S(2)}) %copy-start.7) | copy-done | bytes 536
  2.7 0.0 copy-start.8
  2.7 0.1 copy.13.ids_b
  2.8 0.6 %copy-done.8 = f32[1,64,2]{1,2,0:T(2,128)S(1)} copy-done((f32[1,64,2]{1,2,0:T(2,128)S(1)}, f32[1,64,2]{1,2,0:T(2,128)}, u32[]{:S(2)}) %copy-start.8) | copy-done | bytes 536
  3.3 0.1 copy.14.gates_b
  3.4 0.0 copy-start
  3.4 1.2 %copy-done = bf16[1,4096,128]{2,1,0:T(8,128)(2,1)S(1)} copy-done((bf16[1,4096,128]{2,1,0:T(8,128)(2,1)S(1)}, bf16[1,4096,128]{2,1,0:T(8,128)(2,1)}, u32[]{:S(2)}) %copy-start) | copy-done | bytes 1048600
  4.7 0.0 copy-start.1
  4.7 1.2 %copy-done.1 = bf16[1,128,4096]{2,1,0:T(8,128)(2,1)S(1)} copy-done((bf16[1,128,4096]{2,1,0:T(8,128)(2,1)S(1)}, bf16[1,128,4096]{2,1,0:T(8,128)(2,1)}, u32[]{:S(2)}) %copy-start.1) | copy-done | bytes 1048600
  5.9 0.0 copy-start.2
  5.9 1.0 %copy-done.2 = bf16[1,64,4096]{2,1,0:T(8,128)(2,1)S(1)} copy-done((bf16[1,64,4096]{2,1,0:T(8,128)(2,1)S(1)}, bf16[1,64,4096]{2,1,0:T(8,128)(2,1)}, u32[]{:S(2)}) %copy-start.2) | copy-done | bytes 524312
  6.9 0.0 copy-start.3
  6.9 1.0 %copy-done.3 = bf16[1,64,4096]{2,1,0:T(8,128)(2,1)S(1)} copy-done((bf16[1,64,4096]{2,1,0:T(8,128)(2,1)S(1)}, bf16[1,64,4096]{2,1,0:T(8,128)(2,1)}, u32[]{:S(2)}) %copy-start.3) | copy-done | bytes 524312
  8.0 0.0 copy-start.4
  8.0 1.0 %copy-done.4 = bf16[1,64,4096]{2,1,0:T(8,128)(2,1)S(1)} copy-done((bf16[1,64,4096]{2,1,0:T(8,128)(2,1)S(1)}, bf16[1,64,4096]{2,1,0:T(8,128)(2,1)}, u32[]{:S(2)}) %copy-start.4) | copy-done | bytes 524312
  9.0 43.9 %shard_map.104 = (bf16[64,4096]{1,0:T(8,128)(2,1)S(1)}, bf16[64,4096]{1,0:T(8,128)(2,1)S(1)}) custom-call(s32[64,2]{1,0:T(8,128)S(1)} %copy.11.ids_f, f32[64,2]{1,0:T(8,128)S(1)} %copy.12.gates_f, s32[64,2]{1,0:T(8,128)S(1)} %copy.13.ids_b, f32[64,2]{1,0:T(8,128)S(1)} %copy.14.gates_b, bf16[64,4096]{1,0:T(8,128)(2,1)S(1)} %bitcast.15, ...), custom_call_target="tpu_custom_call" | custom-call | tf_op jit(solution)/shard_map/pallas_call | solution.py:480
  53.0 0.8 %copy.17 = bf16[1,64,4096]{2,1,0:T(8,128)(2,1)} copy(bf16[1,64,4096]{2,1,0:T(8,128)(2,1)S(1)} %bitcast.14) | data formatting | bytes 1048576
  53.8 0.8 %copy.18 = bf16[1,64,4096]{2,1,0:T(8,128)(2,1)} copy(bf16[1,64,4096]{2,1,0:T(8,128)(2,1)S(1)} %bitcast.13) | data formatting | bytes 1048576
Async XLA Ops:
  0.6 0.7 %copy-start.5 = (s32[1,64,2]{1,2,0:T(2,128)S(1)}, s32[1,64,2]{1,2,0:T(2,128)}, u32[]{:S(2)}) copy-start(s32[1,64,2]{1,2,0:T(2,128)} %param.12) | copy-start | bytes 1540
  1.3 0.7 %copy-start.6 = (f32[1,64,2]{1,2,0:T(2,128)S(1)}, f32[1,64,2]{1,2,0:T(2,128)}, u32[]{:S(2)}) copy-start(f32[1,64,2]{1,2,0:T(2,128)} %param.13) | copy-start | bytes 1540
  2.0 0.7 %copy-start.7 = (s32[1,64,2]{1,2,0:T(2,128)S(1)}, s32[1,64,2]{1,2,0:T(2,128)}, u32[]{:S(2)}) copy-start(s32[1,64,2]{1,2,0:T(2,128)} %param.14) | copy-start | bytes 1540
  2.7 0.7 %copy-start.8 = (f32[1,64,2]{1,2,0:T(2,128)S(1)}, f32[1,64,2]{1,2,0:T(2,128)}, u32[]{:S(2)}) copy-start(f32[1,64,2]{1,2,0:T(2,128)} %param.15) | copy-start | bytes 1540
  3.4 1.2 %copy-start = (bf16[1,4096,128]{2,1,0:T(8,128)(2,1)S(1)}, bf16[1,4096,128]{2,1,0:T(8,128)(2,1)}, u32[]{:S(2)}) copy-start(bf16[1,4096,128]{2,1,0:T(8,128)(2,1)} %param.16) | copy-start | bytes 3145732
  4.7 1.2 %copy-start.1 = (bf16[1,128,4096]{2,1,0:T(8,128)(2,1)S(1)}, bf16[1,128,4096]{2,1,0:T(8,128)(2,1)}, u32[]{:S(2)}) copy-start(bf16[1,128,4096]{2,1,0:T(8,128)(2,1)} %param.17) | copy-start | bytes 3145732
  5.9 1.0 %copy-start.2 = (bf16[1,64,4096]{2,1,0:T(8,128)(2,1)S(1)}, bf16[1,64,4096]{2,1,0:T(8,128)(2,1)}, u32[]{:S(2)}) copy-start(bf16[1,64,4096]{2,1,0:T(8,128)(2,1)} %param.9) | copy-start | bytes 1572868
  6.9 1.0 %copy-start.3 = (bf16[1,64,4096]{2,1,0:T(8,128)(2,1)S(1)}, bf16[1,64,4096]{2,1,0:T(8,128)(2,1)}, u32[]{:S(2)}) copy-start(bf16[1,64,4096]{2,1,0:T(8,128)(2,1)} %param.10) | copy-start | bytes 1572868
  8.0 1.0 %copy-start.4 = (bf16[1,64,4096]{2,1,0:T(8,128)(2,1)S(1)}, bf16[1,64,4096]{2,1,0:T(8,128)(2,1)}, u32[]{:S(2)}) copy-start(bf16[1,64,4096]{2,1,0:T(8,128)(2,1)} %param.11) | copy-start | bytes 1572868

commit v2 on v1

--- a/solution.py
+++ b/solution.py
@@ -152,10 +152,10 @@
 def exchange_kernel(
     planes,
     wire,
-    ids_f,
-    gates_f,
-    ids_b,
-    gates_b,
+    ids_f_hbm,
+    gates_f_hbm,
+    ids_b_hbm,
+    gates_b_hbm,
     handoff,
     saved,
     cotangent,
@@ -182,6 +182,12 @@
     z_send,
     z_recv,
     own_sum,
+    ids_f,
+    gates_f,
+    ids_b,
+    gates_b,
+    scatter,
+    gate_wide,
     local_sem,
     send_sem,
     recv_sem,
@@ -204,6 +210,15 @@
     partners = [other_segment, sibling, across] + mates[1:]
     for partner in partners:
         pl.semaphore_signal(barrier, inc=1, device_id=partner, device_id_type=MESH)
+
+    tables = [
+        pltpu.make_async_copy(source, target, local_sem.at[4 + i])
+        for i, (source, target) in enumerate(
+            [(ids_f_hbm, ids_f), (gates_f_hbm, gates_f), (ids_b_hbm, ids_b), (gates_b_hbm, gates_b)]
+        )
+    ]
+    for table_copy in tables:
+        table_copy.start()
 
     @pl.when(segment == 0)
     def _():
@@ -250,49 +265,37 @@
     reduce_y = [remote(y_send.at[k], y_recv.at[k], across) for k in range(planes)]
     reduce_z = [None] + [remote(z_send.at[k], z_recv.at[k], mates[k]) for k in range(1, planes)]
 
+    for table_copy in tables:
+        table_copy.wait()
+    earlier = jnp.where(
+        lax.broadcasted_iota(jnp.int32, (row_count, row_count), 0)
+        < lax.broadcasted_iota(jnp.int32, (row_count, row_count), 1),
+        1.0,
+        0.0,
+    ).astype(jnp.bfloat16)
+
     def ranks(ids, gates):
-        first, second = ids[:, 0:1] == 0, ids[:, 1:2] == 0
+        first, second = ids[0:1, :] == 0, ids[1:2, :] == 0
         member = jnp.where(first | second, 1.0, 0.0)
-        gate = jnp.where(first, gates[:, 0:1], 0.0) + jnp.where(second, gates[:, 1:2], 0.0)
-        earlier = lax.broadcasted_iota(jnp.int32, (row_count, row_count), 1) < lax.broadcasted_iota(
-            jnp.int32, (row_count, row_count), 0
-        )
-        wide = jnp.broadcast_to(member, (row_count, LANES))
-        rank = jnp.dot(
-            jnp.where(earlier, 1.0, 0.0).astype(jnp.bfloat16),
-            wide.astype(jnp.bfloat16),
-            preferred_element_type=jnp.float32,
-        )
-        return wide, rank.astype(jnp.int32), jnp.broadcast_to(gate, (row_count, LANES))
-
-    lane = lax.broadcasted_iota(jnp.int32, (row_count, LANES), 1)
-
-    def placed(member, rank, offset, at=lane):
-        slot = at - offset
+        gate = jnp.where(first, gates[0:1, :], 0.0) + jnp.where(second, gates[1:2, :], 0.0)
+        wide = jnp.broadcast_to(member, (BLOCK, row_count))
+        rank = jnp.dot(wide.astype(jnp.bfloat16), earlier, preferred_element_type=jnp.float32)
+        return wide, rank.astype(jnp.int32), gate
+
+    slot_row = lax.broadcasted_iota(jnp.int32, (BLOCK, row_count), 0)
+
+    def placed(member, rank, offset):
+        slot = slot_row - offset
         fits = (slot == rank) & (slot < CAP) & (slot >= 0)
         return jnp.where(fits, member, 0.0)
 
     member_f, rank_f, gate_f = ranks(ids_f, gates_f)
     member_b, rank_b, gate_b = ranks(ids_b, gates_b)
-    table = (
+    by_slot = (
         placed(member_f, rank_f, 0)
         + placed(member_b, rank_b, CAP)
         + placed(member_b, rank_b, 2 * CAP) * gate_b
     )
-    unit = jnp.where(
-        lax.broadcasted_iota(jnp.int32, (BLOCK, LANES), 0)
-        == lax.broadcasted_iota(jnp.int32, (BLOCK, LANES), 1),
-        1.0,
-        0.0,
-    )
-    by_slot = lax.dot_general(
-        unit,
-        table,
-        (((1,), (1,)), ((), ())),
-        precision=lax.Precision.HIGHEST,
-        preferred_element_type=jnp.float32,
-    )
-    slot_row = lax.broadcasted_iota(jnp.int32, (BLOCK, row_count), 0)
 
     def rows_from(low):
         return jnp.where((slot_row >= low) & (slot_row < low + CAP), by_slot, 0.0)
@@ -326,6 +329,30 @@
         return carry
 
     lax.fori_loop(0, width // turn, transposes, 0)
+    unit = jnp.where(
+        lax.broadcasted_iota(jnp.int32, (row_count, row_count), 0)
+        == lax.broadcasted_iota(jnp.int32, (row_count, row_count), 1),
+        1.0,
+        0.0,
+    )
+    by_row = (((1,), (1,)), ((), ()))
+    for i, (member, rank, offset) in enumerate(
+        [(member_f, rank_f, 0), (member_b, rank_b, CAP), (member_f, rank_f, 2 * CAP), (member_b, rank_b, 2 * CAP)]
+    ):
+        ones = placed(member, rank, offset)
+        scatter[i] = lax.dot_general(
+            unit.astype(jnp.bfloat16),
+            jnp.concatenate([ones, ones], axis=0).astype(jnp.bfloat16),
+            by_row,
+            preferred_element_type=jnp.float32,
+        ).astype(jnp.bfloat16)
+    gate_wide[...] = lax.dot_general(
+        unit,
+        jnp.broadcast_to(gate_f, (LANES, row_count)),
+        by_row,
+        precision=lax.Precision.HIGHEST,
+        preferred_element_type=jnp.float32,
+    )
     response.wait_recv()
     blocks[0, 0, 0] = (own_rows[...] + resp_recv[...].astype(jnp.float32)).astype(jnp.bfloat16)
 
@@ -430,16 +457,9 @@
         if step < planes:
             compute(step)
 
-    lane_half = lane % BLOCK
-
-    def spread_out(member, rank, offset):
-        ones = placed(member, rank, offset, lane_half)
-        return jnp.where(lane < 2 * BLOCK, ones, 0.0)[:, 0 : 2 * BLOCK].astype(jnp.bfloat16)
-
-    heads = jnp.concatenate([spread_out(member_f, rank_f, 0), spread_out(member_b, rank_b, CAP)], axis=0)
-    late_rows_f = spread_out(member_f, rank_f, 2 * CAP)
-    late_rows_b = spread_out(member_b, rank_b, 2 * CAP)
-    gate_wide = jnp.concatenate([gate_f] * (chunk // LANES), axis=1)
+    heads = scatter[0:2].reshape(2 * row_count, 2 * BLOCK)
+    late_rows_f, late_rows_b = scatter[2], scatter[3]
+    wide_gate = jnp.concatenate([gate_wide[...]] * (chunk // LANES), axis=1)
     for k in range(1, planes):
         reduce_z[k].wait_recv()
 
@@ -455,10 +475,10 @@
     for start in range(0, wire, chunk):
         both = halves(start)
         value = jnp.dot(heads, both, preferred_element_type=jnp.float32)
-        out_f[:, start : start + chunk] = (value[0:row_count] * gate_wide).astype(jnp.bfloat16)
+        out_f[:, start : start + chunk] = (value[0:row_count] * wide_gate).astype(jnp.bfloat16)
         out_b[:, start : start + chunk] = value[row_count:].astype(jnp.bfloat16)
         if start < tail_width:
-            value = jnp.dot(late_rows_f, both, preferred_element_type=jnp.float32) * gate_wide
+            value = jnp.dot(late_rows_f, both, preferred_element_type=jnp.float32) * wide_gate
             out_f[:, wire + start : wire + start + chunk] = value.astype(jnp.bfloat16)
         elif start < 2 * tail_width:
             late = wire + start - tail_width
@@ -480,7 +500,7 @@
     mixed, grads = pl.pallas_call(
         functools.partial(exchange_kernel, planes, wire),
         out_shape=[jax.ShapeDtypeStruct((rows, width), bf16)] * 2,
-        in_specs=[vmem] * 4 + [hbm] * 5,
+        in_specs=[hbm] * 9,
         out_specs=[vmem] * 2,
         scratch_shapes=[
             pltpu.VMEM((rows, width), bf16),
@@ -502,18 +522,24 @@
             pltpu.VMEM((planes, BLOCK, wire), bf16),
             pltpu.VMEM((planes, BLOCK, wire), bf16),
             pltpu.VMEM((BLOCK, wire), f32),
-            pltpu.SemaphoreType.DMA((4,)),
+            pltpu.VMEM((2, rows), jnp.int32),
+            pltpu.VMEM((2, rows), f32),
+            pltpu.VMEM((2, rows), jnp.int32),
+            pltpu.VMEM((2, rows), f32),
+            pltpu.VMEM((4, rows, 2 * BLOCK), bf16),
+            pltpu.VMEM((rows, LANES), f32),
+            pltpu.SemaphoreType.DMA((8,)),
             pltpu.SemaphoreType.DMA((copies,)),
             pltpu.SemaphoreType.DMA((copies,)),
         ],
         compiler_params=pltpu.CompilerParams(
-            collective_id=0, has_side_effects=True, vmem_limit_bytes=48 * 1024 * 1024
+            collective_id=0, has_side_effects=True
         ),
     )(
-        ids_forward[0],
-        gates_forward[0],
-        ids_backward[0],
-        gates_backward[0],
+        ids_forward[0].T,
+        gates_forward[0].T,
+        ids_backward[0].T,
+        gates_backward[0].T,
         handoff[0],
         saved_inputs[0],
         cotangent[0],

time: 55 us -> 48.3 us (0.88)
  local copies, waits for them, and re-layouts: 9.96 us -> 2.72 us
  Pallas kernels: 43.9 us -> 44.7 us
    unnamed x20 -> x4, local copies, waits for them, and re-layouts: 9.58 us -> 2.72 us
    pallas_call x1, Pallas kernels: 43.9 us -> 44.7 us  [exchange(): pl.pallas_call(functools.partial(exchange_kernel, planes, wire), out_shap...]
where the time goes in v2:
time: 48.3 us; the launch traced here: 48.1 us
  Pallas kernels  44.7 us (93%)
  local copies, waits for them, and re-layouts  2.72 us (6%)
  between operations  0.65 us (1%)
    pallas_call x1, Pallas kernels, exchange(): pl.pallas_call(functools.partial(exchange_kernel, planes, wire), out_shap...  44.7 us
    unnamed x4, local copies, waits for them, and re-layouts  2.72 us

profile of v2, /device:TPU:0, one launch (start us, length us, event | category | flops | bytes accessed | tf_op | source)
XLA Modules:
  0.0 48.1 jit_solution(3959118095685436636)
XLA Ops:
  0.6 44.7 %shard_map.104 = (bf16[64,4096]{1,0:T(8,128)(2,1)}, bf16[64,4096]{1,0:T(8,128)(2,1)}) custom-call(s32[2,64]{1,0:T(2,128)} %bitcast.26, f32[2,64]{1,0:T(2,128)} %bitcast.27, s32[2,64]{1,0:T(2,128)} %bitcast.28, f32[2,64]{1,0:T(2,128)} %bitcast.29, bf16[64,4096]{1,0:T(8,128)(2,1)} %bitcast.23, bf16[64,4096]{1,0:T(8,128)(2,1)} %bitcast.24, ...), custom_call_target="tpu_custom_call" | custom-call | tf_op jit(solution)/shard_map/pallas_call | solution.py:500
  45.4 0.0 copy-start
  45.4 1.9 %copy.13 = bf16[1,64,4096]{2,1,0:T(8,128)(2,1)} copy(bf16[1,64,4096]{2,1,0:T(8,128)(2,1)} %bitcast.22) | data formatting | bytes 1048576
  47.3 0.0 copy-done
  47.3 0.8 %copy.14 = bf16[1,64,4096]{2,1,0:T(8,128)(2,1)} copy(bf16[1,64,4096]{2,1,0:T(8,128)(2,1)S(1)} %bitcast.21) | data formatting | bytes 1048576
Async XLA Ops:
  45.4 1.9 %copy-start = (bf16[64,4096]{1,0:T(8,128)(2,1)S(1)}, bf16[64,4096]{1,0:T(8,128)(2,1)}, u32[]{:S(2)}) copy-start(bf16[64,4096]{1,0:T(8,128)(2,1)} %get-tuple-element.5) | copy-start | bytes 1572868

commit v3 on v2

--- a/solution.py
+++ b/solution.py
@@ -137,6 +137,7 @@
 
 MESH = pl.DeviceIdType.MESH
 BLOCK = 16
+HALF = 8
 LANES = 128
 
 
@@ -255,15 +256,63 @@
         copy.start()
         started.append(copy)
 
+    plane = expert // 4
+    order = [sorted(range(planes), key=lambda p: (abs(p - z), p)) for z in range(planes)]
+
+    def on_plane(action):
+        for z in range(planes):
+            pl.when(plane == z)(functools.partial(action, z))
+
+    def toward(z, p):
+        return {"expert": expert + (p - z) * 4}
+
     request = remote(req_send, req_recv, other_segment)
     response = remote(resp_send, resp_recv, other_segment)
-    gather_z = [None] + [remote(blocks.at[0, 0, 0], blocks.at[k, 0, 0], mates[k]) for k in range(1, planes)]
     gather_y = [remote(blocks.at[k, 0, 0], blocks.at[k, 1, 0], across) for k in range(planes)]
     gather_c0 = [remote(blocks.at[k, 0, 0], blocks.at[k, 0, 1], sibling) for k in range(planes)]
     gather_c1 = [remote(blocks.at[k, 1, 0], blocks.at[k, 1, 1], sibling) for k in range(planes)]
     reduce_c = [remote(pair_send.at[k], pair_recv.at[k], sibling) for k in range(planes)]
     reduce_y = [remote(y_send.at[k], y_recv.at[k], across) for k in range(planes)]
-    reduce_z = [None] + [remote(z_send.at[k], z_recv.at[k], mates[k]) for k in range(1, planes)]
+    gather_base, reduce_base = count[0], count[0] + planes + 1
+
+    def gather_z(z, k, step):
+        source = order[z][k]
+        slot = order[z + step].index(source)
+        number = gather_base + (planes if k == 0 and step > 0 else k)
+        return pltpu.make_async_remote_copy(
+            src_ref=blocks.at[k, 0, 0],
+            dst_ref=blocks.at[slot, 0, 0],
+            send_sem=send_sem.at[number],
+            recv_sem=recv_sem.at[gather_base + slot],
+            device_id=toward(z, z + step),
+            device_id_type=MESH,
+        )
+
+    def onward(z, k):
+        source = order[z][k]
+        steps = [-1, 1] if source == z else [1 if source < z else -1]
+        return [gather_z(z, k, step) for step in steps if 0 <= z + step < planes]
+
+    def reduce_z(z, k):
+        slot = order[order[z][k]].index(z)
+        return pltpu.make_async_remote_copy(
+            src_ref=z_send.at[k],
+            dst_ref=z_recv.at[slot],
+            send_sem=send_sem.at[reduce_base + k],
+            recv_sem=recv_sem.at[reduce_base + slot],
+            device_id=toward(z, order[z][k]),
+            device_id_type=MESH,
+        )
+
+    def arrival(base, k, buffer):
+        return pltpu.make_async_remote_copy(
+            src_ref=buffer,
+            dst_ref=buffer,
+            send_sem=send_sem.at[base + k],
+            recv_sem=recv_sem.at[base + k],
+            device_id=sibling,
+            device_id_type=MESH,
+        )
 
     for table_copy in tables:
         table_copy.wait()
@@ -291,19 +340,13 @@
 
     member_f, rank_f, gate_f = ranks(ids_f, gates_f)
     member_b, rank_b, gate_b = ranks(ids_b, gates_b)
-    by_slot = (
-        placed(member_f, rank_f, 0)
-        + placed(member_b, rank_b, CAP)
-        + placed(member_b, rank_b, 2 * CAP) * gate_b
-    )
-
-    def rows_from(low):
-        return jnp.where((slot_row >= low) & (slot_row < low + CAP), by_slot, 0.0)
-
-    asked = rows_from((1 - segment) * (2 * CAP))
-    mine = rows_from(segment * (2 * CAP))
-    kept = rows_from(CAP)
-    req_send[...] = jnp.concatenate([asked, jnp.zeros((BLOCK, LANES - row_count), jnp.float32)], axis=1)
+    later = (segment * jnp.ones((), jnp.int32)).astype(jnp.float32)
+    first_f, first_b = placed(member_f, rank_f, 0), placed(member_b, rank_b, 0) * gate_b
+    last_f, last_b = placed(member_f, rank_f, 2 * CAP), placed(member_b, rank_b, 2 * CAP) * gate_b
+    asked = (first_b * (1.0 - later) + first_f * later)[0:HALF]
+    mine = last_f * (1.0 - later) + last_b * later
+    kept = placed(member_b, rank_b, CAP)
+    req_send[...] = jnp.concatenate([asked, jnp.zeros((HALF, LANES - row_count), jnp.float32)], axis=1)
     pl.semaphore_wait(barrier, len(partners))
     begin(request)
 
@@ -354,12 +397,19 @@
         preferred_element_type=jnp.float32,
     )
     response.wait_recv()
-    blocks[0, 0, 0] = (own_rows[...] + resp_recv[...].astype(jnp.float32)).astype(jnp.bfloat16)
+    own_rows[0:HALF, :] = own_rows[0:HALF, :] + resp_recv[...].astype(jnp.float32)
+    blocks[0, 0, 0] = own_rows[...].astype(jnp.bfloat16)
 
     def spread(k):
         if k > 0:
-            gather_z[k].wait_recv()
+            arrival(gather_base, k, blocks.at[k, 0, 0]).wait_recv()
         begin(gather_y[k])
+
+        def pass_on(z):
+            for copy in onward(z, k):
+                copy.start()
+
+        on_plane(pass_on)
         begin(gather_c0[k])
 
     def relay(k):
@@ -386,9 +436,14 @@
             0, width // turn, contract, jnp.zeros((batch, 2 * hidden), jnp.float32), unroll=True
         )
         pre = both[:, 0:hidden]
-        grad_hidden = pltpu.roll(both[:, hidden:], batch - CAP, 0)
+        grad_hidden = both[:, hidden:]
+        grad_hidden = (
+            pltpu.roll(grad_hidden, CAP, 0) * (1.0 - later) + pltpu.roll(grad_hidden, batch - CAP, 0) * later
+        )
         gate = 1.0 / (1.0 + jnp.exp(-pre))
-        forward = jnp.where(place < CAP, pre * gate, 0.0)
+        silu = pre * gate
+        silu = pltpu.roll(silu, batch - 2 * CAP, 0) * (1.0 - later) + silu * later
+        forward = jnp.where(place < CAP, silu, 0.0)
         slope = gate * (1.0 + pre * (1.0 - gate))
         backward = jnp.where((place >= CAP) & (place < 2 * CAP), grad_hidden * slope, 0.0)
         late_f = pltpu.roll(forward, 2 * CAP, 0).astype(jnp.bfloat16)
@@ -440,10 +495,8 @@
             own_sum[...] = total
         else:
             z_send[k] = total.astype(jnp.bfloat16)
-            begin(reduce_z[k])
-
-    for k in range(1, planes):
-        begin(gather_z[k])
+            on_plane(lambda z: reduce_z(z, k).start())
+
     spread(0)
     for step in range(planes + 2):
         if step + 1 < planes:
@@ -461,7 +514,7 @@
     late_rows_f, late_rows_b = scatter[2], scatter[3]
     wide_gate = jnp.concatenate([gate_wide[...]] * (chunk // LANES), axis=1)
     for k in range(1, planes):
-        reduce_z[k].wait_recv()
+        arrival(reduce_base, k, z_recv.at[k]).wait_recv()
 
     def halves(start):
         columns = slice(start, start + chunk)
@@ -487,6 +540,15 @@
     for copy in started:
         copy.wait_send()
 
+    def drain(z):
+        for k in range(planes):
+            for copy in onward(z, k):
+                copy.wait_send()
+            if k > 0:
+                reduce_z(z, k).wait_send()
+
+    on_plane(drain)
+
 
 def exchange(planes, handoff, saved_inputs, cotangent, ids_forward, gates_forward, ids_backward, gates_backward, weight_in, weight_out):
     rows, width = handoff.shape[1:]
@@ -494,7 +556,7 @@
     tiles = width // LANES
     wire = -(-2 * tiles // 3) * LANES
     bf16, f32 = jnp.bfloat16, jnp.float32
-    copies = 2 + 2 * (planes - 1) + 5 * planes
+    copies = 2 + 7 * planes + 1
     vmem = pl.BlockSpec(memory_space=pltpu.VMEM)
     hbm = pl.BlockSpec(memory_space=pl.ANY)
     mixed, grads = pl.pallas_call(
@@ -508,10 +570,10 @@
             pltpu.VMEM((width, 2 * hidden), bf16),
             pltpu.VMEM((2 * hidden, width), bf16),
             pltpu.VMEM((planes, 2, 2, BLOCK, width), bf16),
-            pltpu.VMEM((BLOCK, LANES), f32),
-            pltpu.VMEM((BLOCK, LANES), f32),
-            pltpu.VMEM((BLOCK, width), bf16),
-            pltpu.VMEM((BLOCK, width), bf16),
+            pltpu.VMEM((HALF, LANES), f32),
+            pltpu.VMEM((HALF, LANES), f32),
+            pltpu.VMEM((HALF, width), bf16),
+            pltpu.VMEM((HALF, width), bf16),
             pltpu.VMEM((BLOCK, width), f32),
             pltpu.VMEM((planes, 2, BLOCK, wire), bf16),
             pltpu.VMEM((planes, 2, BLOCK, wire), f32),

time: 48.3 us -> 50.4 us (1.043)
  Pallas kernels: 44.7 us -> 46.8 us
    pallas_call x1, Pallas kernels: 44.7 us -> 46.8 us  [exchange(): pl.pallas_call(functools.partial(exchange_kernel, planes, wire), out_shap...]
where the time goes in v3:
time: 50.4 us; the launch traced here: 50.2 us
  Pallas kernels  46.8 us (93%)
  local copies, waits for them, and re-layouts  2.72 us (5%)
  between operations  0.65 us (1%)
    pallas_call x1, Pallas kernels, exchange(): pl.pallas_call(functools.partial(exchange_kernel, planes, wire), out_shap...  46.8 us
    unnamed x4, local copies, waits for them, and re-layouts  2.72 us

profile of v3, /device:TPU:0, one launch (start us, length us, event | category | flops | bytes accessed | tf_op | source)
XLA Modules:
  0.0 50.2 jit_solution(16036739989468107568)
XLA Ops:
  0.6 46.8 %shard_map.104 = (bf16[64,4096]{1,0:T(8,128)(2,1)}, bf16[64,4096]{1,0:T(8,128)(2,1)}) custom-call(s32[2,64]{1,0:T(2,128)} %bitcast.26, f32[2,64]{1,0:T(2,128)} %bitcast.27, s32[2,64]{1,0:T(2,128)} %bitcast.28, f32[2,64]{1,0:T(2,128)} %bitcast.29, bf16[64,4096]{1,0:T(8,128)(2,1)} %bitcast.23, bf16[64,4096]{1,0:T(8,128)(2,1)} %bitcast.24, ...), custom_call_target="tpu_custom_call" | custom-call | tf_op jit(solution)/shard_map/pallas_call | solution.py:562
  47.5 0.0 copy-start
  47.5 1.9 %copy.13 = bf16[1,64,4096]{2,1,0:T(8,128)(2,1)} copy(bf16[1,64,4096]{2,1,0:T(8,128)(2,1)} %bitcast.22) | data formatting | bytes 1048576
  49.4 0.0 copy-done
  49.4 0.8 %copy.14 = bf16[1,64,4096]{2,1,0:T(8,128)(2,1)} copy(bf16[1,64,4096]{2,1,0:T(8,128)(2,1)S(1)} %bitcast.21) | data formatting | bytes 1048576
Async XLA Ops:
  47.5 1.9 %copy-start = (bf16[64,4096]{1,0:T(8,128)(2,1)S(1)}, bf16[64,4096]{1,0:T(8,128)(2,1)}, u32[]{:S(2)}) copy-start(bf16[64,4096]{1,0:T(8,128)(2,1)} %get-tuple-element.5) | copy-start | bytes 1572868

commit v4 on v2

--- a/solution.py
+++ b/solution.py
@@ -137,6 +137,8 @@
 
 MESH = pl.DeviceIdType.MESH
 BLOCK = 16
+HALF = 8
+PARTS = 2
 LANES = 128
 
 
@@ -257,13 +259,36 @@
 
     request = remote(req_send, req_recv, other_segment)
     response = remote(resp_send, resp_recv, other_segment)
-    gather_z = [None] + [remote(blocks.at[0, 0, 0], blocks.at[k, 0, 0], mates[k]) for k in range(1, planes)]
-    gather_y = [remote(blocks.at[k, 0, 0], blocks.at[k, 1, 0], across) for k in range(planes)]
-    gather_c0 = [remote(blocks.at[k, 0, 0], blocks.at[k, 0, 1], sibling) for k in range(planes)]
-    gather_c1 = [remote(blocks.at[k, 1, 0], blocks.at[k, 1, 1], sibling) for k in range(planes)]
-    reduce_c = [remote(pair_send.at[k], pair_recv.at[k], sibling) for k in range(planes)]
-    reduce_y = [remote(y_send.at[k], y_recv.at[k], across) for k in range(planes)]
-    reduce_z = [None] + [remote(z_send.at[k], z_recv.at[k], mates[k]) for k in range(1, planes)]
+
+    def cuts(total):
+        tiles = total // LANES
+        edges = [tiles * i // PARTS * LANES for i in range(PARTS + 1)]
+        return [slice(low, high) for low, high in zip(edges[:-1], edges[1:])]
+
+    wide_cuts, wire_cuts = cuts(width), cuts(wire)
+
+    def gather(source, target, device):
+        return [
+            remote(blocks.at[(*source, slice(None), cut)], blocks.at[(*target, slice(None), cut)], device)
+            for cut in wide_cuts
+        ]
+
+    gather_z = [None] + [gather((0, 0, 0), (k, 0, 0), mates[k]) for k in range(1, planes)]
+    gather_y = [gather((k, 0, 0), (k, 1, 0), across) for k in range(planes)]
+    gather_c0 = [gather((k, 0, 0), (k, 0, 1), sibling) for k in range(planes)]
+    gather_c1 = [gather((k, 1, 0), (k, 1, 1), sibling) for k in range(planes)]
+    reduce_c = [
+        [remote(pair_send.at[k, :, :, cut], pair_recv.at[k, :, :, cut], sibling) for cut in wire_cuts]
+        for k in range(planes)
+    ]
+    reduce_y = [
+        [remote(y_send.at[k, :, cut], y_recv.at[k, :, cut], across) for cut in wire_cuts]
+        for k in range(planes)
+    ]
+    reduce_z = [None] + [
+        [remote(z_send.at[k, :, cut], z_recv.at[k, :, cut], mates[k]) for cut in wire_cuts]
+        for k in range(1, planes)
+    ]
 
     for table_copy in tables:
         table_copy.wait()
@@ -291,19 +316,13 @@
 
     member_f, rank_f, gate_f = ranks(ids_f, gates_f)
     member_b, rank_b, gate_b = ranks(ids_b, gates_b)
-    by_slot = (
-        placed(member_f, rank_f, 0)
-        + placed(member_b, rank_b, CAP)
-        + placed(member_b, rank_b, 2 * CAP) * gate_b
-    )
-
-    def rows_from(low):
-        return jnp.where((slot_row >= low) & (slot_row < low + CAP), by_slot, 0.0)
-
-    asked = rows_from((1 - segment) * (2 * CAP))
-    mine = rows_from(segment * (2 * CAP))
-    kept = rows_from(CAP)
-    req_send[...] = jnp.concatenate([asked, jnp.zeros((BLOCK, LANES - row_count), jnp.float32)], axis=1)
+    later = (segment * jnp.ones((), jnp.int32)).astype(jnp.float32)
+    first_f, first_b = placed(member_f, rank_f, 0), placed(member_b, rank_b, 0) * gate_b
+    last_f, last_b = placed(member_f, rank_f, 2 * CAP), placed(member_b, rank_b, 2 * CAP) * gate_b
+    asked = (first_b * (1.0 - later) + first_f * later)[0:HALF]
+    mine = last_f * (1.0 - later) + last_b * later
+    kept = placed(member_b, rank_b, CAP)
+    req_send[...] = jnp.concatenate([asked, jnp.zeros((HALF, LANES - row_count), jnp.float32)], axis=1)
     pl.semaphore_wait(barrier, len(partners))
     begin(request)
 
@@ -354,25 +373,29 @@
         preferred_element_type=jnp.float32,
     )
     response.wait_recv()
-    blocks[0, 0, 0] = (own_rows[...] + resp_recv[...].astype(jnp.float32)).astype(jnp.bfloat16)
+    own_rows[0:HALF, :] = own_rows[0:HALF, :] + resp_recv[...].astype(jnp.float32)
+    blocks[0, 0, 0] = own_rows[...].astype(jnp.bfloat16)
 
     def spread(k):
-        if k > 0:
-            gather_z[k].wait_recv()
-        begin(gather_y[k])
-        begin(gather_c0[k])
+        for part in range(PARTS):
+            if k > 0:
+                gather_z[k][part].wait_recv()
+            begin(gather_y[k][part])
+            begin(gather_c0[k][part])
 
     def relay(k):
-        gather_y[k].wait_recv()
-        begin(gather_c1[k])
+        for part in range(PARTS):
+            gather_y[k][part].wait_recv()
+            begin(gather_c1[k][part])
 
     batch = 4 * BLOCK
     place = lax.broadcasted_iota(jnp.int32, (batch, hidden), 0) % BLOCK
     chunk = 256 if tail_width % 256 == 0 and wire % 256 == 0 else LANES
 
     def compute(k):
-        gather_c0[k].wait_recv()
-        gather_c1[k].wait_recv()
+        for part in range(PARTS):
+            gather_c0[k][part].wait_recv()
+            gather_c1[k][part].wait_recv()
 
         def contract(step, total):
             piece = pl.ds(pl.multiple_of(step * turn, turn), turn)
@@ -386,9 +409,14 @@
             0, width // turn, contract, jnp.zeros((batch, 2 * hidden), jnp.float32), unroll=True
         )
         pre = both[:, 0:hidden]
-        grad_hidden = pltpu.roll(both[:, hidden:], batch - CAP, 0)
+        grad_hidden = both[:, hidden:]
+        grad_hidden = (
+            pltpu.roll(grad_hidden, CAP, 0) * (1.0 - later) + pltpu.roll(grad_hidden, batch - CAP, 0) * later
+        )
         gate = 1.0 / (1.0 + jnp.exp(-pre))
-        forward = jnp.where(place < CAP, pre * gate, 0.0)
+        silu = pre * gate
+        silu = pltpu.roll(silu, batch - 2 * CAP, 0) * (1.0 - later) + silu * later
+        forward = jnp.where(place < CAP, silu, 0.0)
         slope = gate * (1.0 + pre * (1.0 - gate))
         backward = jnp.where((place >= CAP) & (place < 2 * CAP), grad_hidden * slope, 0.0)
         late_f = pltpu.roll(forward, 2 * CAP, 0).astype(jnp.bfloat16)
@@ -425,43 +453,53 @@
         lax.fori_loop(0, tail_width // chunk, pieces, 0, unroll=True)
         for start in range(2 * tail_width, wire, chunk):
             put(start, product(start))
-        begin(reduce_c[k])
+        for copy in reduce_c[k]:
+            begin(copy)
 
     def join_pair(k):
-        reduce_c[k].wait_recv()
-        y_send[k] = (pair_keep[k, 1] + pair_recv[k, 1].astype(jnp.float32)).astype(jnp.bfloat16)
-        begin(reduce_y[k])
-        y_keep[k] = pair_keep[k, 0] + pair_recv[k, 0].astype(jnp.float32)
+        for part, cut in enumerate(wire_cuts):
+            reduce_c[k][part].wait_recv()
+            sent = pair_keep[k, 1, :, cut] + pair_recv[k, 1, :, cut].astype(jnp.float32)
+            y_send[k, :, cut] = sent.astype(jnp.bfloat16)
+            begin(reduce_y[k][part])
+            y_keep[k, :, cut] = pair_keep[k, 0, :, cut] + pair_recv[k, 0, :, cut].astype(jnp.float32)
 
     def join_plane(k):
-        reduce_y[k].wait_recv()
-        total = y_keep[k] + y_recv[k].astype(jnp.float32)
-        if k == 0:
-            own_sum[...] = total
-        else:
-            z_send[k] = total.astype(jnp.bfloat16)
-            begin(reduce_z[k])
+        for part, cut in enumerate(wire_cuts):
+            reduce_y[k][part].wait_recv()
+            total = y_keep[k, :, cut] + y_recv[k, :, cut].astype(jnp.float32)
+            if k == 0:
+                own_sum[:, cut] = total
+            else:
+                z_send[k, :, cut] = total.astype(jnp.bfloat16)
+                begin(reduce_z[k][part])
 
     for k in range(1, planes):
-        begin(gather_z[k])
+        for copy in gather_z[k]:
+            begin(copy)
     spread(0)
-    for step in range(planes + 2):
-        if step + 1 < planes:
-            spread(step + 1)
-        if step < planes:
-            relay(step)
-        if 0 <= step - 1 < planes:
-            join_pair(step - 1)
-        if 0 <= step - 2 < planes:
-            join_plane(step - 2)
-        if step < planes:
-            compute(step)
+    last = planes - 1
+    for step in range(last):
+        spread(step + 1)
+        if step == last - 1:
+            for k in range(step):
+                join_pair(k)
+        relay(step)
+        compute(step)
+    join_pair(last - 1)
+    relay(last)
+    join_plane(0)
+    compute(last)
+    join_pair(last)
+    for k in range(1, planes):
+        join_plane(k)
 
     heads = scatter[0:2].reshape(2 * row_count, 2 * BLOCK)
     late_rows_f, late_rows_b = scatter[2], scatter[3]
     wide_gate = jnp.concatenate([gate_wide[...]] * (chunk // LANES), axis=1)
     for k in range(1, planes):
-        reduce_z[k].wait_recv()
+        for copy in reduce_z[k]:
+            copy.wait_recv()
 
     def halves(start):
         columns = slice(start, start + chunk)
@@ -494,7 +532,7 @@
     tiles = width // LANES
     wire = -(-2 * tiles // 3) * LANES
     bf16, f32 = jnp.bfloat16, jnp.float32
-    copies = 2 + 2 * (planes - 1) + 5 * planes
+    copies = 2 + PARTS * (2 * (planes - 1) + 5 * planes)
     vmem = pl.BlockSpec(memory_space=pltpu.VMEM)
     hbm = pl.BlockSpec(memory_space=pl.ANY)
     mixed, grads = pl.pallas_call(
@@ -508,10 +546,10 @@
             pltpu.VMEM((width, 2 * hidden), bf16),
             pltpu.VMEM((2 * hidden, width), bf16),
             pltpu.VMEM((planes, 2, 2, BLOCK, width), bf16),
-            pltpu.VMEM((BLOCK, LANES), f32),
-            pltpu.VMEM((BLOCK, LANES), f32),
-            pltpu.VMEM((BLOCK, width), bf16),
-            pltpu.VMEM((BLOCK, width), bf16),
+            pltpu.VMEM((HALF, LANES), f32),
+            pltpu.VMEM((HALF, LANES), f32),
+            pltpu.VMEM((HALF, width), bf16),
+            pltpu.VMEM((HALF, width), bf16),
             pltpu.VMEM((BLOCK, width), f32),
             pltpu.VMEM((planes, 2, BLOCK, wire), bf16),
             pltpu.VMEM((planes, 2, BLOCK, wire), f32),

time: 48.3 us -> 47.2 us (0.977)
  Pallas kernels: 44.7 us -> 43.7 us
    pallas_call x1, Pallas kernels: 44.7 us -> 43.7 us  [exchange(): pl.pallas_call(functools.partial(exchange_kernel, planes, wire), out_shap...]
where the time goes in v4:
time: 47.2 us; the launch traced here: 47 us
  Pallas kernels  43.7 us (93%)
  local copies, waits for them, and re-layouts  2.72 us (6%)
  between operations  0.65 us (1%)
    pallas_call x1, Pallas kernels, exchange(): pl.pallas_call(functools.partial(exchange_kernel, planes, wire), out_shap...  43.7 us
    unnamed x4, local copies, waits for them, and re-layouts  2.72 us

profile of v4, /device:TPU:0, one launch (start us, length us, event | category | flops | bytes accessed | tf_op | source)
XLA Modules:
  0.0 47.0 jit_solution(2262054048768695469)
XLA Ops:
  0.6 43.7 %shard_map.104 = (bf16[64,4096]{1,0:T(8,128)(2,1)}, bf16[64,4096]{1,0:T(8,128)(2,1)}) custom-call(s32[2,64]{1,0:T(2,128)} %bitcast.26, f32[2,64]{1,0:T(2,128)} %bitcast.27, s32[2,64]{1,0:T(2,128)} %bitcast.28, f32[2,64]{1,0:T(2,128)} %bitcast.29, bf16[64,4096]{1,0:T(8,128)(2,1)} %bitcast.23, bf16[64,4096]{1,0:T(8,128)(2,1)} %bitcast.24, ...), custom_call_target="tpu_custom_call" | custom-call | tf_op jit(solution)/shard_map/pallas_call | solution.py:538
  44.3 0.0 copy-start
  44.3 1.9 %copy.13 = bf16[1,64,4096]{2,1,0:T(8,128)(2,1)} copy(bf16[1,64,4096]{2,1,0:T(8,128)(2,1)} %bitcast.22) | data formatting | bytes 1048576
  46.2 0.0 copy-done
  46.2 0.8 %copy.14 = bf16[1,64,4096]{2,1,0:T(8,128)(2,1)} copy(bf16[1,64,4096]{2,1,0:T(8,128)(2,1)S(1)} %bitcast.21) | data formatting | bytes 1048576
Async XLA Ops:
  44.3 1.9 %copy-start = (bf16[64,4096]{1,0:T(8,128)(2,1)S(1)}, bf16[64,4096]{1,0:T(8,128)(2,1)}, u32[]{:S(2)}) copy-start(bf16[64,4096]{1,0:T(8,128)(2,1)} %get-tuple-element.5) | copy-start | bytes 1572868
